TPU v7x, 256 devices: a whole 4x4x8 slice. The times are simulated.
256 devices in a mesh: space: 64 (over z_hi, y, x, core), dp: 4 (over z_lo).
Axes of the slice: x: 4, y: 4, z: 8 (z_hi: 2, z_lo: 4; z = z_hi * 4 + z_lo), core: 2. Of those that a mesh axis runs over, the one named last changes fastest.
Arguments:
- activations: bfloat16 [4, 256, 16, 16, 128], P('dp', 'space'), may hold values from -100 to 100
- upstream: bfloat16 [4, 256, 16, 16, 128], P('dp', 'space'), may hold values from -100 to 100
- kernel_weight: bfloat16 [27, 128, 128], replicated, may hold values from -0.109375 to 0.109375
- patch_inverse: float32 [27, 128, 3456], P(None, 'space'), may hold values from -0.1 to 1.6, as said below
- output_inverse: float32 [128, 128], replicated, may hold values from -0.1 to 1.6, as said below
Outputs:
- activated: bfloat16 [4, 256, 16, 16, 128], P('dp', 'space')
- input_grad: bfloat16 [4, 256, 16, 16, 128], P('dp', 'space')
- patch_factor: float32 [128, 63, 128], P('space', None, 'dp')
- output_factor: float32 [128, 128], replicated
- precond_grad: float32 [27, 128, 128], P(None, 'space')
Inputs may be any that keep to these rules, and one draw needn't show every extreme that they name: Symmetric as a 3456 x 3456 matrix whose row o * 128 + c is patch_inverse[o, c, :]. `output_inverse`: symmetric.
All inputs are finite; a program needn't handle non-finite values.
Results may differ from a plain program's by a relative error of at most 0.0015.
The roundings to bfloat16 on the way count: a program that leaves them out, or rounds other values in their place, can miss the bound.
Values may be sent and summed in bfloat16 or wider, within the bound.
A program may use at most 128 MiB of HBM per device.

v0:
```python
import functools

import jax
import jax.numpy as jnp
from jax import lax
from jax.experimental import pallas as pl
from jax.experimental.pallas import tpu as pltpu
from jax.sharding import PartitionSpec as P

F32 = jnp.float32
BF16 = jnp.bfloat16
TOTAL = 262144.0
NT = (((1,), (1,)), ((), ()))
HIGHEST = lax.Precision.HIGHEST


def dot(a, b):
    return jnp.dot(a, b, preferred_element_type=F32)


def tap_shift(offset):
    return (offset // 9 - 1, offset // 3 % 3 - 1, offset % 3 - 1)


def step_kernel(
    act,
    up,
    kw,
    pinv,
    oinv,
    activated,
    input_grad,
    patch_factor,
    output_factor,
    precond,
    halo_a,
    halo_s,
    slope,
    ext_a,
    ext_s,
    left,
    left12,
    slope_t,
    prod_l,
    got_lc,
    out_l1,
    got_l1,
    sum_l1,
    out_l2,
    got_l2,
    out_l3,
    got_l3,
    prod_w,
    got_wc,
    out_w1,
    got_w1,
    out_w2,
    got_w2,
    out_w3,
    got_w3,
    weights,
    inverse,
    part_p,
    got_p,
    send_sem,
    recv_sem,
):
    space = lax.axis_index("space")
    quarter = lax.axis_index("dp")
    core = lax.rem(space, 2)
    col = lax.rem(space // 2, 4)
    row = lax.rem(space // 8, 4)
    half = space // 32
    depth = half * 4 + quarter
    other = 1 - core

    def device(half, row, col, core, quarter):
        return {"space": ((half * 4 + row) * 4 + col) * 2 + core, "dp": quarter}

    sibling = device(half, row, col, other, quarter)
    following = {"space": lax.rem(space + 1, 64), "dp": quarter}
    preceding = {"space": lax.rem(space + 63, 64), "dp": quarter}
    far = {"space": lax.rem(space + 2 * core + 63, 64), "dp": quarter}

    def along_x(t):
        at = lax.rem(col + t, 4)
        return at, device(half, row, at, core, quarter)

    def along_y(t):
        at = lax.rem(row + t, 4)
        return at, device(half, at, col, core, quarter)

    def along_z(t):
        at = lax.rem(depth + t, 8)
        return at, device(at // 4, row, col, core, lax.rem(at, 4))

    def along_dp(t):
        at = lax.rem(quarter + t, 4)
        return at, device(half, row, col, core, at)

    count = [0]

    def send(src, dst, to):
        n = count[0]
        count[0] += 1
        copy = pltpu.make_async_remote_copy(
            src_ref=src,
            dst_ref=dst,
            send_sem=send_sem.at[n],
            recv_sem=recv_sem.at[n],
            device_id=to,
            device_id_type=pl.DeviceIdType.MESH,
        )
        copy.start()
        sent.append(copy)
        return copy

    sent = []

    partners = [sibling, far]
    partners += [along_x(t)[1] for t in (1, 2, 3)]
    partners += [along_y(t)[1] for t in (1, 2, 3)]
    partners += [along_z(t)[1] for t in range(1, 8)]
    barrier = pltpu.get_barrier_semaphore()
    for partner in partners:
        pl.semaphore_signal(
            barrier, inc=1, device_id=partner, device_id_type=pl.DeviceIdType.MESH
        )
    pl.semaphore_wait(barrier, len(partners))

    before = send(act.at[3], halo_a.at[0], following)
    after = send(act.at[0], halo_a.at[1], preceding)

    r = lax.broadcasted_iota(jnp.int32, (128, 128), 0)
    c = lax.broadcasted_iota(jnp.int32, (128, 128), 1)

    def picked(first, second):
        chan = (
            (r & 1)
            + 2 * ((r >> 6) & 1)
            + first * ((r >> 4) & 3)
            + second * ((r >> 2) & 3)
            + 64 * ((r >> 1) & 1)
        )
        return jnp.where(c == chan, 1.0, 0.0).astype(BF16)

    orders = (picked(4, 16), picked(16, 4))
    unit = jnp.where(c == r, 1.0, 0.0).astype(BF16)

    def turned(order, plane):
        return lax.dot_general(order, plane, NT, preferred_element_type=F32).astype(BF16)

    def place_a(plane, at):
        wide = plane.astype(F32).reshape(16, 16, 128)
        for dx in range(-2, 3):
            moved = plane
            if dx:
                moved = pltpu.roll(wide, (-dx) % 16, 1).reshape(256, 128).astype(BF16)
            ext_a[dx + 2, at, 32:288, :] = moved
            ext_a[dx + 2, at, 0:32, :] = moved[224:256]
            ext_a[dx + 2, at, 288:320, :] = moved[0:32]
        for part in range(2):
            left[part, :, at * 256 : (at + 1) * 256] = turned(orders[part], plane)

    def place_s(plane, at):
        wide = plane.astype(F32).reshape(16, 16, 128)
        for dx in range(-1, 2):
            moved = plane
            if dx:
                moved = pltpu.roll(wide, (-dx) % 16, 1).reshape(256, 128).astype(BF16)
            ext_s[dx + 1, at, 16:272, :] = moved
            ext_s[dx + 1, at, 0:16, :] = moved[240:256]
            ext_s[dx + 1, at, 272:288, :] = moved[0:16]

    def rows_a(first, dy, dx):
        return ext_a[dx + 2, first : first + 4, (2 + dy) * 16 : (2 + dy) * 16 + 256, :].reshape(
            1024, 128
        )

    for z in range(4):
        place_a(act[z], z + 1)

    prod_l[1, 31] = jnp.zeros((128, 128), F32)
    prod_w[3, 6] = jnp.zeros((128, 128), F32)
    inverse[:, 3456:3584] = jnp.zeros((56, 128), F32)
    inverse[48:56, :] = jnp.zeros((8, 3584), F32)
    for o in range(27):
        inverse[2 * o : 2 * o + 2, 0:3456] = pinv[o]

    for k in range(13):
        m = k + 62
        part, slot = (0, 25 + k) if k < 7 else (1, 18 + k)
        prod_l[part, slot] = dot(
            left[part, :, 256:1280], rows_a(1, m // 5 % 5 - 2, m % 5 - 2)
        )

    before.wait_recv()
    after.wait_recv()
    place_a(halo_a[0], 0)
    place_a(halo_a[1], 5)
    left12[0:128, :] = left[0, :, 256:1280]
    left12[128:256, :] = left[1, :, 0:1024]

    kernel_rows = kw[...].reshape(27 * 128, 128)
    for z in (0, 3, 1, 2):
        taps = []
        for o in range(27):
            dz, dy, dx = tap_shift(o)
            taps.append(ext_a[dx + 2, z + 1 + dz, (2 + dy) * 16 : (2 + dy) * 16 + 256, :])
        pre = dot(jnp.concatenate(taps, axis=1), kernel_rows)
        logistic = jax.nn.sigmoid(pre)
        activated[z] = (pre * logistic).astype(BF16)
        sloped = (up[z].astype(F32) * logistic * (1.0 + pre * (1.0 - logistic))).astype(BF16)
        slope[z] = sloped
        slope_t[:, z * 256 : (z + 1) * 256] = turned(unit, sloped)
        if z == 3:
            before_s = send(slope.at[3], halo_s.at[0], following)
            after_s = send(slope.at[0], halo_s.at[1], preceding)

    for o in range(27):
        dz, dy, dx = tap_shift(o)
        prod_w[o // 7, o % 7] = dot(slope_t[...], rows_a(1 + dz, dy, dx))
    own = dot(slope_t[...], slope[...].reshape(1024, 128))
    for d in range(4):
        prod_w[d, 7] = own

    theirs = pl.ds(pl.multiple_of(other * 64, 64), 64)
    mine = pl.ds(pl.multiple_of(core * 64, 64), 64)
    wc = send(prod_w.at[:, :, theirs, :], got_wc, sibling)

    pairs = [(dy, dx) for dy in range(-2, 3) for dx in range(-2, 3)]

    def lag_block(first, last):
        for s in range(first, last):
            both = dot(left12[...], rows_a(2, *pairs[s]))
            prod_l[0, s] = both[0:128]
            prod_l[1, s] = both[128:256]

    lag_block(0, 12)

    wc.wait_recv()
    out_w1[...] = (prod_w[:, :, mine, :] + got_wc[...]).astype(out_w1.dtype)
    firsts = (col, row)
    first_axis = (along_x, along_y)
    second_axis = (along_y, along_x)
    seconds = (row, col)

    w1 = []
    for part in range(2):
        for t in range(1, 4):
            at, to = first_axis[part](t)
            w1.append(
                send(
                    out_w1.at[:, 4 * part : 4 * part + 4, pl.ds(pl.multiple_of(at * 16, 16), 16), :],
                    got_w1.at[part, t - 1],
                    to,
                )
            )

    lag_block(12, 25)
    lc = send(prod_l.at[:, :, theirs, :], got_lc, sibling)

    before_s.wait_recv()
    after_s.wait_recv()
    for z in range(4):
        place_s(slope[z], z + 1)
    place_s(halo_s[0], 0)
    place_s(halo_s[1], 5)

    for copy in w1:
        copy.wait_recv()
    w2 = []
    for part in range(2):
        kept = pl.ds(pl.multiple_of(firsts[part] * 16, 16), 16)
        tall = pl.ds(pl.multiple_of(core * 64 + firsts[part] * 16, 16), 16)
        for b in range(4):
            out_w2[part, b] = (
                prod_w[:, 4 * part + b, tall, :]
                + got_wc[:, 4 * part + b, kept, :]
                + got_w1[part, 0, :, b].astype(F32)
                + got_w1[part, 1, :, b].astype(F32)
                + got_w1[part, 2, :, b].astype(F32)
            )
        for t in range(1, 4):
            at, to = second_axis[part](t)
            w2.append(send(out_w2.at[part, at], got_w2.at[part, t - 1], to))

    kernel_cols = jnp.concatenate([kw[o] for o in range(27)], axis=1)

    def back(z):
        taps = []
        for o in range(27):
            dz, dy, dx = tap_shift(o)
            taps.append(ext_s[1 - dx, z + 1 - dz, (1 - dy) * 16 : (1 - dy) * 16 + 256, :])
        grad = lax.dot_general(
            jnp.concatenate(taps, axis=1), kernel_cols, NT, preferred_element_type=F32
        )
        input_grad[z] = grad.astype(BF16)

    back(0)

    lc.wait_recv()
    for part in range(2):
        out_l1[part] = (prod_l[part, :, mine, :] + got_lc[part]).astype(BF16)
    l1 = []
    for part in range(2):
        for t in range(1, 4):
            at, to = first_axis[part](t)
            l1.append(
                send(
                    out_l1.at[part, :, pl.ds(pl.multiple_of(at * 16, 16), 16), :],
                    got_l1.at[part, t - 1],
                    to,
                )
            )

    for copy in w2:
        copy.wait_recv()
    for part in range(2):
        total = out_w2[part, seconds[part]]
        for t in range(3):
            total = total + got_w2[part, t]
        for d in range(4):
            out_w3[d, part] = total[d]
    got_w3[depth] = out_w3[quarter]
    w3 = []
    for t in range(1, 8):
        at, to = along_z(t)
        w3.append(send(out_w3.at[lax.rem(at, 4)], got_w3.at[depth], to))

    back(1)

    for copy in w3:
        copy.wait_recv()
    reduced = got_w3[0]
    for z in range(1, 8):
        reduced = reduced + got_w3[z]
    rows0 = pl.ds(pl.multiple_of(core * 64 + col * 16, 16), 16)
    rows1 = pl.ds(pl.multiple_of(core * 64 + row * 16, 16), 16)
    weights[row, rows0, :] = reduced[0]
    weights[4 + col, rows1, :] = reduced[1]
    g1 = []
    for t in range(1, 4):
        g1.append(send(weights.at[row, rows0, :], weights.at[row, rows0, :], along_y(t)[1]))
        g1.append(send(weights.at[4 + col, rows1, :], weights.at[4 + col, rows1, :], along_x(t)[1]))

    back(2)

    for copy in g1:
        copy.wait_recv()
    g2 = []
    for t in range(1, 4):
        g2.append(send(weights.at[0:4, rows0, :], weights.at[0:4, rows0, :], along_x(t)[1]))
        g2.append(send(weights.at[4:8, rows1, :], weights.at[4:8, rows1, :], along_y(t)[1]))

    back(3)

    for copy in l1:
        copy.wait_recv()
    l2 = []
    for part in range(2):
        kept = pl.ds(pl.multiple_of(firsts[part] * 16, 16), 16)
        tall = pl.ds(pl.multiple_of(core * 64 + firsts[part] * 16, 16), 16)
        total = prod_l[part, :, tall, :] + got_lc[part, :, kept, :]
        for t in range(3):
            total = total + got_l1[part, t].astype(F32)
        sum_l1[part] = total.reshape(512, 128)
        for b in range(4):
            for n in range(4):
                for g in range(4):
                    out_l2[part, b, n, 8 * g : 8 * g + 8, :] = sum_l1[
                        part, pl.ds(4 * b + n + 128 * g, 8, stride=16), :
                    ]
        for t in range(1, 4):
            at, to = second_axis[part](t)
            l2.append(send(out_l2.at[part, at], got_l2.at[part, t - 1], to))

    for copy in g2:
        copy.wait_recv()
    g3 = send(weights.at[:, mine, :], weights.at[:, mine, :], sibling)

    for copy in l2:
        copy.wait_recv()
    lane = lax.broadcasted_iota(jnp.int32, (32, 128), 1) // 32
    totals = []
    for part in range(2):
        total = out_l2[part, seconds[part]]
        for t in range(3):
            total = total + got_l2[part, t]
        totals.append(total)
    for h in range(2):
        groups = [totals[part][2 * h + i] for part in range(2) for i in range(2)]
        for q in range(4):
            packed = jnp.zeros((32, 128), F32)
            for j in range(4):
                shift = (32 * (j - q)) % 128
                piece = pltpu.roll(groups[j], shift, 1) if shift else groups[j]
                packed = jnp.where(lane == j, piece, packed)
            out_l3[4 * h + q] = packed
    l3 = []
    for t in range(1, 8):
        at, to = along_z(t)
        l3.append(send(out_l3.at[at], got_l3.at[t - 1], to))

    g3.wait_recv()
    cut = pl.ds(pl.multiple_of(quarter * 896, 128), 896)
    gathered = jnp.concatenate([weights[b] for b in range(7)], axis=1)
    part_p[...] = lax.dot_general(
        inverse[:, cut], gathered, NT, preferred_element_type=F32, precision=HIGHEST
    )
    got_p[quarter] = part_p[...]
    pp = []
    for t in range(1, 4):
        pp.append(send(part_p, got_p.at[quarter], along_dp(t)[1]))
    output_factor[...] = weights[7] * (1.0 / TOTAL)

    for copy in l3:
        copy.wait_recv()
    final = out_l3[depth]
    for t in range(7):
        final = final + got_l3[t]
    final = final * (1.0 / TOTAL)
    for i in range(2):
        for part in range(2):
            j = 2 * part + i
            piece = (pltpu.roll(final, (-32 * j) % 128, 1) if j else final)[:, 0:32]
            if part == 0:
                patch_factor[i, 13:38, :] = piece[0:25]
                patch_factor[i, 0:7, :] = piece[25:32]
            else:
                patch_factor[i, 38:63, :] = piece[0:25]
                patch_factor[i, 7:13, :] = piece[25:31]

    for copy in pp:
        copy.wait_recv()
    product = got_p[0] + got_p[1] + got_p[2] + got_p[3]
    product = jnp.dot(
        product, oinv[...], preferred_element_type=F32, precision=HIGHEST
    ) * (1.0 / TOTAL)
    for o in range(27):
        precond[o] = product[2 * o : 2 * o + 2]

    for copy in sent:
        copy.wait_send()


def per_device(activations, upstream, kernel_weight, patch_inverse, output_inverse):
    vmem = pl.BlockSpec(memory_space=pltpu.VMEM)
    scratch = [
        ((2, 256, 128), BF16),
        ((2, 256, 128), BF16),
        ((4, 256, 128), BF16),
        ((5, 6, 320, 128), BF16),
        ((3, 6, 288, 128), BF16),
        ((2, 128, 1536), BF16),
        ((256, 1024), BF16),
        ((128, 1024), BF16),
        ((2, 32, 128, 128), F32),
        ((2, 32, 64, 128), F32),
        ((2, 32, 64, 128), BF16),
        ((2, 3, 32, 16, 128), BF16),
        ((2, 512, 128), F32),
        ((2, 4, 4, 32, 128), F32),
        ((2, 3, 4, 32, 128), F32),
        ((8, 32, 128), F32),
        ((7, 32, 128), F32),
        ((4, 8, 128, 128), F32),
        ((4, 8, 64, 128), F32),
        ((4, 8, 64, 128), F32),
        ((2, 3, 4, 4, 16, 128), F32),
        ((2, 4, 4, 16, 128), F32),
        ((2, 3, 4, 16, 128), F32),
        ((4, 2, 16, 128), F32),
        ((8, 2, 16, 128), F32),
        ((8, 128, 128), F32),
        ((56, 3584), F32),
        ((56, 128), F32),
        ((4, 56, 128), F32),
    ]
    outs = pl.pallas_call(
        step_kernel,
        out_shape=(
            jax.ShapeDtypeStruct((4, 256, 128), BF16),
            jax.ShapeDtypeStruct((4, 256, 128), BF16),
            jax.ShapeDtypeStruct((2, 63, 32), F32),
            jax.ShapeDtypeStruct((128, 128), F32),
            jax.ShapeDtypeStruct((27, 2, 128), F32),
        ),
        in_specs=[vmem] * 5,
        out_specs=[vmem] * 5,
        scratch_shapes=[pltpu.VMEM(shape, dtype) for shape, dtype in scratch]
        + [pltpu.SemaphoreType.DMA((72,)), pltpu.SemaphoreType.DMA((72,))],
        compiler_params=pltpu.CompilerParams(
            collective_id=0, has_side_effects=True, vmem_limit_bytes=56 * 1024 * 1024
        ),
        name="step_kernel",
    )(
        activations.reshape(4, 256, 128),
        upstream.reshape(4, 256, 128),
        kernel_weight,
        patch_inverse,
        output_inverse,
    )
    activated, input_grad, patch_factor, output_factor, precond = outs
    return (
        activated.reshape(activations.shape),
        input_grad.reshape(activations.shape),
        patch_factor,
        output_factor,
        precond,
    )


def solution(mesh):
    return jax.shard_map(
        per_device,
        mesh=mesh,
        in_specs=(
            P("dp", "space", None, None, None),
            P("dp", "space", None, None, None),
            P(),
            P(None, "space", None),
            P(),
        ),
        out_specs=(
            P("dp", "space", None, None, None),
            P("dp", "space", None, None, None),
            P("space", None, "dp"),
            P(),
            P(None, "space", None),
        ),
        check_vma=False,
    )
```

profile of v0, /device:TPU:1, one launch (start us, length us, event | category | flops | bytes accessed | tf_op | source)
XLA Modules:
  0.0 69.0 jit_solution(11664843952535336081)
XLA Ops:
  0.6 62.9 %step_kernel.1 = (bf16[4,256,128]{2,1,0:T(8,128)(2,1)}, bf16[4,256,128]{2,1,0:T(8,128)(2,1)}, f32[2,63,32]{2,1,0:T(8,128)}, f32[128,128]{1,0:T(8,128)}, f32[27,2,128]{2,1,0:T(2,128)}) custom-call(bf16[4,256,128]{2,1,0:T(8,128)(2,1)} %bitcast.6, bf16[4,256,128]{2,1,0:T(8,128)(2,1)} %bitcast.7, bf16[27,128,128]{2,1,0:T(8,128)(2,1)} %kw.1, ...), custom_call_target="tpu_custom_call" | custom-call | tf_op jit(solution)/shard_map/step_kernel/pallas_call | solution.py:480
  63.5 1.5 %copy.10 = f32[2,63,32]{1,2,0:T(8,128)} copy(f32[2,63,32]{2,1,0:T(8,128)} %get-tuple-element.17) | data formatting | bytes 32256
  65.0 0.0 copy-start
  65.0 1.7 %copy.15 = bf16[1,4,16,16,128]{4,3,2,1,0:T(8,128)(2,1)} copy(bf16[1,4,16,16,128]{4,3,2,1,0:T(8,128)(2,1)} %bitcast.5) | data formatting | bytes 524288
  66.7 0.0 copy-done
  66.7 0.0 copy-start.1
  66.7 0.7 %copy.16 = bf16[1,4,16,16,128]{4,3,2,1,0:T(8,128)(2,1)} copy(bf16[1,4,16,16,128]{4,3,2,1,0:T(8,128)(2,1)S(1)} %bitcast.4) | data formatting | bytes 524288
  67.4 0.2 copy-done.1
  67.6 0.0 copy-start.2
  67.6 0.6 copy.17
  68.2 0.1 copy-done.2
  68.4 0.6 copy.18
Async XLA Ops:
  65.0 1.7 %copy-start = (bf16[4,256,128]{2,1,0:T(8,128)(2,1)S(1)}, bf16[4,256,128]{2,1,0:T(8,128)(2,1)}, u32[]{:S(2)}) copy-start(bf16[4,256,128]{2,1,0:T(8,128)(2,1)} %get-tuple-element.11) | copy-start | bytes 786436
  66.7 0.9 %copy-start.1 = (f32[128,128]{1,0:T(8,128)S(1)}, f32[128,128]{1,0:T(8,128)}, u32[]{:S(2)}) copy-start(f32[128,128]{1,0:T(8,128)} %get-tuple-element.28) | copy-start | bytes 196612
  67.6 0.7 %copy-start.2 = (f32[27,2,128]{2,1,0:T(2,128)S(1)}, f32[27,2,128]{2,1,0:T(2,128)}, u32[]{:S(2)}) copy-start(f32[27,2,128]{2,1,0:T(2,128)} %get-tuple-element.29) | copy-start | bytes 82948
where the time goes:
time: 69.4 us; the launch traced here: 69 us
  Pallas kernels  62.9 us (91%)
  local copies, waits for them, and re-layouts  5.46 us (8%)
    pallas_call x1, Pallas kernels, per_device(): pl.pallas_call(step_kernel, out_shape=(jax.ShapeDtypeStruct((4, 256, 128)...  62.9 us
    unnamed x11, local copies, waits for them, and re-layouts  5.46 us

commit v1 on v0

v1 whole, which is shorter than its diff:
```python
import functools

import jax
import jax.numpy as jnp
from jax import lax
from jax.experimental import pallas as pl
from jax.experimental.pallas import tpu as pltpu
from jax.sharding import PartitionSpec as P

F32 = jnp.float32
BF16 = jnp.bfloat16
TOTAL = 262144.0
NT = (((1,), (1,)), ((), ()))
HIGHEST = lax.Precision.HIGHEST


def dot(a, b):
    return jnp.dot(a, b, preferred_element_type=F32)


def tap_shift(offset):
    return (offset // 9 - 1, offset // 3 % 3 - 1, offset % 3 - 1)


def step_kernel(
    act_hbm,
    up_hbm,
    kw_hbm,
    pinv_hbm,
    oinv_hbm,
    activated_hbm,
    input_grad_hbm,
    patch_factor,
    output_factor,
    precond,
    act,
    up,
    kw,
    pinv,
    oinv,
    activated,
    input_grad,
    halo_a,
    halo_s,
    slope,
    ext_a,
    ext_s,
    left,
    left12,
    slope_t,
    prod_l,
    got_lc,
    out_l1,
    got_l1,
    sum_l1,
    out_l2,
    got_l2,
    out_l3,
    got_l3,
    prod_w,
    got_wc,
    out_w1,
    got_w1,
    out_w3,
    got_w3,
    weights,
    inverse,
    part_p,
    got_p,
    local_sem,
    send_sem,
    recv_sem,
):
    space = lax.axis_index("space")
    quarter = lax.axis_index("dp")
    core = lax.rem(space, 2)
    col = lax.rem(space // 2, 4)
    row = lax.rem(space // 8, 4)
    half = space // 32
    depth = half * 4 + quarter
    other = 1 - core

    def device(half, row, col, core, quarter):
        return {"space": ((half * 4 + row) * 4 + col) * 2 + core, "dp": quarter}

    sibling = device(half, row, col, other, quarter)
    following = {"space": lax.rem(space + 1, 64), "dp": quarter}
    preceding = {"space": lax.rem(space + 63, 64), "dp": quarter}
    far = {"space": lax.rem(space + 2 * core + 63, 64), "dp": quarter}

    def along_x(t):
        at = lax.rem(col + t, 4)
        return at, device(half, row, at, core, quarter)

    def along_y(t):
        at = lax.rem(row + t, 4)
        return at, device(half, at, col, core, quarter)

    def in_plane(t):
        at_y = lax.rem(row + t // 4, 4)
        at_x = lax.rem(col + t % 4, 4)
        return at_y, at_x, device(half, at_y, at_x, core, quarter)

    def along_z(t):
        at = lax.rem(depth + t, 8)
        return at, device(at // 4, row, col, core, lax.rem(at, 4))

    def along_dp(t):
        at = lax.rem(quarter + t, 4)
        return at, device(half, row, col, core, at)

    def sixteen(at):
        return pl.ds(pl.multiple_of(at * 16, 16), 16)

    count = [0, 0]
    sent = []
    moved_out = []

    def send(src, dst, to):
        n = count[0]
        count[0] += 1
        copy = pltpu.make_async_remote_copy(
            src_ref=src,
            dst_ref=dst,
            send_sem=send_sem.at[n],
            recv_sem=recv_sem.at[n],
            device_id=to,
            device_id_type=pl.DeviceIdType.MESH,
        )
        copy.start()
        sent.append(copy)
        return copy

    def move(src, dst):
        n = count[1]
        count[1] += 1
        copy = pltpu.make_async_copy(src, dst, local_sem.at[n])
        copy.start()
        return copy

    partners = [sibling, far]
    partners += [in_plane(t)[2] for t in range(1, 16)]
    partners += [along_z(t)[1] for t in range(1, 8)]
    barrier = pltpu.get_barrier_semaphore()
    for partner in partners:
        pl.semaphore_signal(
            barrier, inc=1, device_id=partner, device_id_type=pl.DeviceIdType.MESH
        )

    act_in = move(act_hbm, act)
    kw_in = move(kw_hbm, kw)
    up_in = move(up_hbm, up)
    pinv_in = move(pinv_hbm, pinv)
    oinv_in = move(oinv_hbm, oinv)

    r = lax.broadcasted_iota(jnp.int32, (128, 128), 0)
    c = lax.broadcasted_iota(jnp.int32, (128, 128), 1)

    def picked(first, second):
        chan = (
            (r & 1)
            + 2 * ((r >> 6) & 1)
            + first * ((r >> 4) & 3)
            + second * ((r >> 2) & 3)
            + 64 * ((r >> 1) & 1)
        )
        return jnp.where(c == chan, 1.0, 0.0).astype(BF16)

    orders = (picked(4, 16), picked(16, 4))
    unit = jnp.where(c == r, 1.0, 0.0).astype(BF16)

    def turned(order, plane):
        return lax.dot_general(order, plane, NT, preferred_element_type=F32).astype(BF16)

    def place_a(plane, at):
        wide = plane.astype(F32).reshape(16, 16, 128)
        for dx in range(-2, 3):
            moved = plane
            if dx:
                moved = pltpu.roll(wide, (-dx) % 16, 1).reshape(256, 128).astype(BF16)
            ext_a[dx + 2, at, 32:288, :] = moved
            ext_a[dx + 2, at, 0:32, :] = moved[224:256]
            ext_a[dx + 2, at, 288:320, :] = moved[0:32]
        for part in range(2):
            left[part, :, at * 256 : (at + 1) * 256] = turned(orders[part], plane)

    def place_s(plane, at):
        wide = plane.astype(F32).reshape(16, 16, 128)
        for dx in range(-1, 2):
            moved = plane
            if dx:
                moved = pltpu.roll(wide, (-dx) % 16, 1).reshape(256, 128).astype(BF16)
            ext_s[dx + 1, at, 16:272, :] = moved
            ext_s[dx + 1, at, 0:16, :] = moved[240:256]
            ext_s[dx + 1, at, 272:288, :] = moved[0:16]

    def rows_a(first, dy, dx, planes=4):
        return ext_a[
            dx + 2, first : first + planes, (2 + dy) * 16 : (2 + dy) * 16 + 256, :
        ].reshape(planes * 256, 128)

    def ends_a(dz, dy, dx):
        return jnp.concatenate([rows_a(1 + dz, dy, dx, 1), rows_a(4 + dz, dy, dx, 1)], axis=0)

    prod_l[1, 31] = jnp.zeros((128, 128), F32)
    prod_w[3, 1, 2] = jnp.zeros((128, 128), F32)
    inverse[:, 3456:3584] = jnp.zeros((56, 128), F32)
    inverse[48:56, :] = jnp.zeros((8, 3584), F32)

    act_in.wait()
    for z in range(4):
        place_a(act[z], z + 1)
    for k in range(13):
        m = k + 62
        part, slot = (0, 25 + k) if k < 7 else (1, 18 + k)
        prod_l[part, slot] = dot(
            left[part, :, 256:1280], rows_a(1, m // 5 % 5 - 2, m % 5 - 2)
        )

    kw_in.wait()
    up_in.wait()

    def forward(z):
        taps = []
        for o in range(27):
            dz, dy, dx = tap_shift(o)
            taps.append(ext_a[dx + 2, z + 1 + dz, (2 + dy) * 16 : (2 + dy) * 16 + 256, :])
        pre = dot(jnp.concatenate(taps, axis=1), kw[...].reshape(27 * 128, 128))
        logistic = jax.nn.sigmoid(pre)
        activated[z] = (pre * logistic).astype(BF16)
        sloped = (up[z].astype(F32) * logistic * (1.0 + pre * (1.0 - logistic))).astype(BF16)
        slope[z] = sloped
        slope_t[:, z * 256 : (z + 1) * 256] = turned(unit, sloped)

    forward(1)
    forward(2)

    pl.semaphore_wait(barrier, len(partners))
    before = send(act.at[3], halo_a.at[0], following)
    after = send(act.at[0], halo_a.at[1], preceding)

    theirs = pl.ds(pl.multiple_of(other * 64, 64), 64)
    mine = pl.ds(pl.multiple_of(core * 64, 64), 64)
    firsts = (col, row)
    seconds = (row, col)
    first_axis = (along_x, along_y)
    second_axis = (along_y, along_x)

    def swap_l(first, last):
        return send(
            prod_l.at[:, first:last, theirs, :], got_lc.at[:, first:last], sibling
        )

    def spread_l(first, last):
        copies = []
        for part in range(2):
            out_l1[part, first:last] = (
                prod_l[part, first:last, mine, :] + got_lc[part, first:last]
            ).astype(BF16)
            for t in range(1, 4):
                at, to = first_axis[part](t)
                copies.append(
                    send(
                        out_l1.at[part, first:last, sixteen(at), :],
                        got_l1.at[part, t - 1, first:last],
                        to,
                    )
                )
        return copies

    early_c = swap_l(25, 32)

    def blocks(d):
        for b in range(7):
            if 7 * d + b < 27:
                yield b, tap_shift(7 * d + b)

    inner_t = slope_t[:, 256:768]
    for d in range(4):
        for b, (dz, dy, dx) in blocks(d):
            prod_w[d, b // 4, b % 4] = dot(inner_t, rows_a(2 + dz, dy, dx, 2))
    inner_own = dot(inner_t, slope[1:3].reshape(512, 128))

    early_c.wait_recv()
    l1 = spread_l(25, 32)

    pinv_in.wait()
    for o in range(27):
        inverse[2 * o : 2 * o + 2, 0:3456] = pinv[o]

    before.wait_recv()
    place_a(halo_a[0], 0)
    after.wait_recv()
    place_a(halo_a[1], 5)
    forward(3)
    forward(0)
    before_s = send(slope.at[3], halo_s.at[0], following)
    after_s = send(slope.at[0], halo_s.at[1], preceding)
    activated_out = move(activated, activated_hbm)

    outer_t = jnp.concatenate([slope_t[:, 0:256], slope_t[:, 768:1024]], axis=1)
    own = inner_own + dot(outer_t, jnp.concatenate([slope[0], slope[3]], axis=0))
    wc = []
    for d in range(4):
        prod_w[d, 1, 3] = own
        for b, (dz, dy, dx) in blocks(d):
            prod_w[d, b // 4, b % 4] += dot(outer_t, ends_a(dz, dy, dx))
        wc.append(send(prod_w.at[d, :, :, theirs, :], got_wc.at[d], sibling))

    left12[0:128, :] = left[0, :, 256:1280]
    left12[128:256, :] = left[1, :, 0:1024]
    pairs = [(dy, dx) for dy in range(-2, 3) for dx in range(-2, 3)]

    def lag_block(first, last):
        for s in range(first, last):
            both = dot(left12[...], rows_a(2, *pairs[s]))
            prod_l[0, s] = both[0:128]
            prod_l[1, s] = both[128:256]
        return swap_l(first, last)

    lc = [lag_block(0, 12)]

    for copy in wc:
        copy.wait_recv()
    out_w1[...] = (prod_w[:, :, :, mine, :] + got_wc[...]).astype(BF16)
    w1 = []
    for t in range(1, 16):
        at_y, at_x, to = in_plane(t)
        w1.append(send(out_w1.at[:, :, at_y, sixteen(at_x), :], got_w1.at[t - 1], to))

    lc.append(lag_block(12, 25))
    for copy in lc:
        copy.wait_recv()
    l1 += spread_l(0, 25)

    for z in range(4):
        place_s(slope[z], z + 1)
    before_s.wait_recv()
    after_s.wait_recv()
    place_s(halo_s[0], 0)
    place_s(halo_s[1], 5)

    kernel_cols = jnp.concatenate([kw[o] for o in range(27)], axis=1)

    def back(z):
        taps = []
        for o in range(27):
            dz, dy, dx = tap_shift(o)
            taps.append(ext_s[1 - dx, z + 1 - dz, (1 - dy) * 16 : (1 - dy) * 16 + 256, :])
        grad = lax.dot_general(
            jnp.concatenate(taps, axis=1), kernel_cols, NT, preferred_element_type=F32
        )
        input_grad[z] = grad.astype(BF16)

    back(0)

    for copy in w1:
        copy.wait_recv()
    tall = sixteen(core * 4 + col)
    total_w = prod_w[:, :, row, tall, :] + got_wc[:, :, row, sixteen(col), :]
    for t in range(15):
        total_w = total_w + got_w1[t].astype(F32)
    out_w3[...] = total_w
    got_w3[depth] = out_w3[quarter]
    w3 = []
    for t in range(1, 8):
        at, to = along_z(t)
        w3.append(send(out_w3.at[lax.rem(at, 4)], got_w3.at[depth], to))

    back(1)

    for copy in l1:
        copy.wait_recv()
    l2 = []
    for part in range(2):
        kept = sixteen(firsts[part])
        high = sixteen(core * 4 + firsts[part])
        total = prod_l[part, :, high, :] + got_lc[part, :, kept, :]
        for t in range(3):
            total = total + got_l1[part, t].astype(F32)
        sum_l1[part] = total.reshape(512, 128)
        for b in range(4):
            for n in range(4):
                for g in range(4):
                    out_l2[part, b, n, 8 * g : 8 * g + 8, :] = sum_l1[
                        part, pl.ds(4 * b + n + 128 * g, 8, stride=16), :
                    ]
        for t in range(1, 4):
            at, to = second_axis[part](t)
            l2.append(send(out_l2.at[part, at], got_l2.at[part, t - 1], to))

    back(2)

    for copy in w3:
        copy.wait_recv()
    reduced = got_w3[0]
    for z in range(1, 8):
        reduced = reduced + got_w3[z]
    weights[:, row, tall, :] = reduced
    g1 = []
    for t in range(1, 16):
        piece = weights.at[:, row, tall, :]
        g1.append(send(piece, piece, in_plane(t)[2]))

    back(3)
    input_grad_out = move(input_grad, input_grad_hbm)

    for copy in l2:
        copy.wait_recv()
    group = c[0:32] // 32
    totals = []
    for part in range(2):
        total = out_l2[part, seconds[part]]
        for t in range(3):
            total = total + got_l2[part, t]
        totals.append(total)
    for h in range(2):
        groups = [totals[part][2 * h + i] for part in range(2) for i in range(2)]
        for q in range(4):
            packed = jnp.zeros((32, 128), F32)
            for j in range(4):
                shift = (32 * (j - q)) % 128
                piece = pltpu.roll(groups[j], shift, 1) if shift else groups[j]
                packed = jnp.where(group == j, piece, packed)
            out_l3[4 * h + q] = packed
    l3 = []
    for t in range(1, 8):
        at, to = along_z(t)
        l3.append(send(out_l3.at[at], got_l3.at[t - 1], to))

    for copy in g1:
        copy.wait_recv()
    g3 = send(weights.at[:, :, mine, :], weights.at[:, :, mine, :], sibling)
    g3.wait_recv()
    cut = pl.ds(pl.multiple_of(quarter * 896, 128), 896)
    gathered = jnp.concatenate([weights[b // 4, b % 4] for b in range(7)], axis=1)
    part_p[...] = lax.dot_general(
        inverse[:, cut], gathered, NT, preferred_element_type=F32, precision=HIGHEST
    )
    got_p[quarter] = part_p[...]
    pp = []
    for t in range(1, 4):
        pp.append(send(part_p, got_p.at[quarter], along_dp(t)[1]))
    output_factor[...] = weights[1, 3] * (1.0 / TOTAL)

    for copy in l3:
        copy.wait_recv()
    final = out_l3[depth]
    for t in range(7):
        final = final + got_l3[t]
    final = final * (1.0 / TOTAL)
    flipped = jnp.concatenate([final, jnp.zeros((96, 128), F32)], axis=0).T
    lane = c[0:32]
    for i in range(2):
        one = flipped[32 * i : 32 * i + 32]
        two = flipped[64 + 32 * i : 96 + 32 * i]
        piece = jnp.where(lane < 7, pltpu.roll(one, 103, 1), pltpu.roll(two, 110, 1))
        piece = jnp.where(lane < 13, piece, pltpu.roll(one, 13, 1))
        piece = jnp.where(lane < 38, piece, pltpu.roll(two, 38, 1))
        patch_factor[i] = piece[:, 0:63]

    oinv_in.wait()
    for copy in pp:
        copy.wait_recv()
    product = got_p[0] + got_p[1] + got_p[2] + got_p[3]
    product = jnp.dot(
        product, oinv[...], preferred_element_type=F32, precision=HIGHEST
    ) * (1.0 / TOTAL)
    for o in range(27):
        precond[o] = product[2 * o : 2 * o + 2]

    activated_out.wait()
    input_grad_out.wait()
    for copy in sent:
        copy.wait_send()


def hand_on(*refs):
    sources, results, stops, sems = refs[:5], refs[5:10], refs[10:15], refs[15]
    arrivals = []
    for n in range(5):
        copy = pltpu.make_async_copy(sources[n], stops[n], sems.at[n])
        copy.start()
        arrivals.append(copy)
    departures = []
    for n in range(5):
        arrivals[n].wait()
        copy = pltpu.make_async_copy(stops[n], results[n], sems.at[5 + n])
        copy.start()
        departures.append(copy)
    for copy in departures:
        copy.wait()


def per_device(activations, upstream, kernel_weight, patch_inverse, output_inverse):
    vmem = pl.BlockSpec(memory_space=pltpu.VMEM)
    hbm = pl.BlockSpec(memory_space=pl.ANY)
    scratch = [
        ((4, 256, 128), BF16),
        ((4, 256, 128), BF16),
        ((27, 128, 128), BF16),
        ((27, 2, 3456), F32),
        ((128, 128), F32),
        ((4, 256, 128), BF16),
        ((4, 256, 128), BF16),
        ((2, 256, 128), BF16),
        ((2, 256, 128), BF16),
        ((4, 256, 128), BF16),
        ((5, 6, 320, 128), BF16),
        ((3, 6, 288, 128), BF16),
        ((2, 128, 1536), BF16),
        ((256, 1024), BF16),
        ((128, 1024), BF16),
        ((2, 32, 128, 128), F32),
        ((2, 32, 64, 128), F32),
        ((2, 32, 64, 128), BF16),
        ((2, 3, 32, 16, 128), BF16),
        ((2, 512, 128), F32),
        ((2, 4, 4, 32, 128), F32),
        ((2, 3, 4, 32, 128), F32),
        ((8, 32, 128), F32),
        ((7, 32, 128), F32),
        ((4, 2, 4, 128, 128), F32),
        ((4, 2, 4, 64, 128), F32),
        ((4, 2, 4, 64, 128), BF16),
        ((15, 4, 2, 16, 128), BF16),
        ((4, 2, 16, 128), F32),
        ((8, 2, 16, 128), F32),
        ((2, 4, 128, 128), F32),
        ((56, 3584), F32),
        ((56, 128), F32),
        ((4, 56, 128), F32),
    ]
    shapes = (
        jax.ShapeDtypeStruct((4, 256, 128), BF16),
        jax.ShapeDtypeStruct((4, 256, 128), BF16),
        jax.ShapeDtypeStruct((2, 32, 63), F32),
        jax.ShapeDtypeStruct((128, 128), F32),
        jax.ShapeDtypeStruct((27, 2, 128), F32),
    )
    outs = pl.pallas_call(
        step_kernel,
        out_shape=shapes,
        in_specs=[hbm] * 5,
        out_specs=[hbm, hbm, vmem, vmem, vmem],
        scratch_shapes=[pltpu.VMEM(shape, dtype) for shape, dtype in scratch]
        + [
            pltpu.SemaphoreType.DMA((8,)),
            pltpu.SemaphoreType.DMA((96,)),
            pltpu.SemaphoreType.DMA((96,)),
        ],
        compiler_params=pltpu.CompilerParams(
            collective_id=0, has_side_effects=True, vmem_limit_bytes=60 * 1024 * 1024
        ),
        name="step_kernel",
    )(
        activations.reshape(4, 256, 128),
        upstream.reshape(4, 256, 128),
        kernel_weight,
        patch_inverse,
        output_inverse,
    )
    outs = pl.pallas_call(
        hand_on,
        out_shape=shapes,
        in_specs=[hbm] * 5,
        out_specs=[hbm] * 5,
        scratch_shapes=[pltpu.VMEM(shape.shape, shape.dtype) for shape in shapes]
        + [pltpu.SemaphoreType.DMA((10,))],
        compiler_params=pltpu.CompilerParams(vmem_limit_bytes=60 * 1024 * 1024),
        name="hand_on",
    )(*outs)
    activated, input_grad, patch_factor, output_factor, precond = outs
    return (
        activated.reshape(activations.shape),
        input_grad.reshape(activations.shape),
        jnp.transpose(patch_factor, (0, 2, 1)),
        output_factor,
        precond,
    )


def solution(mesh):
    return jax.shard_map(
        per_device,
        mesh=mesh,
        in_specs=(
            P("dp", "space", None, None, None),
            P("dp", "space", None, None, None),
            P(),
            P(None, "space", None),
            P(),
        ),
        out_specs=(
            P("dp", "space", None, None, None),
            P("dp", "space", None, None, None),
            P("space", None, "dp"),
            P(),
            P(None, "space", None),
        ),
        check_vma=False,
    )
```

time: 69.4 us -> 57 us (0.82)
  Pallas kernels: 62.9 us -> 56.1 us
  local copies, waits for them, and re-layouts: 5.46 us -> 0 us
    pallas_call x1 -> x2, Pallas kernels: 62.9 us -> 56.1 us  [the longest x1 54.2 us: per_device(): pl.pallas_call(step_kernel, out_shape=shapes, in_specs=[hbm] * 5, out_spe...]
    unnamed x11 -> x0, local copies, waits for them, and re-layouts: 5.46 us -> none
where the time goes in v1:
time: 57 us; the launch traced here: 56.9 us
  Pallas kernels  56.1 us (98%)
  between operations  0.8 us (1%)
    pallas_call x1, Pallas kernels, per_device(): pl.pallas_call(step_kernel, out_shape=shapes, in_specs=[hbm] * 5, out_spe...  54.2 us
    pallas_call x1, Pallas kernels, per_device(): pl.pallas_call(hand_on, out_shape=shapes, in_specs=[hbm] * 5, out_specs=[...  1.85 us

profile of v1, /device:TPU:1, one launch (start us, length us, event | category | flops | bytes accessed | tf_op | source)
XLA Modules:
  0.0 56.9 jit_solution(8168079112915852553)
XLA Ops:
  0.6 54.2 %step_kernel.1 = (bf16[4,256,128]{2,1,0:T(8,128)(2,1)}, bf16[4,256,128]{2,1,0:T(8,128)(2,1)}, f32[2,32,63]{2,1,0:T(8,128)}, f32[128,128]{1,0:T(8,128)}, f32[27,2,128]{2,1,0:T(2,128)}) custom-call(bf16[4,256,128]{2,1,0:T(8,128)(2,1)} %bitcast.5, bf16[4,256,128]{2,1,0:T(8,128)(2,1)} %bitcast.6, bf16[27,128,128]{2,1,0:T(8,128)(2,1)} %kw_hbm.1, ...), custom_call_target="tpu_custom_call" | custom-call | tf_op jit(solution)/shard_map/step_kernel/pallas_call | solution.py:541
  54.9 1.9 %hand_on.1 = (bf16[4,256,128]{2,1,0:T(8,128)(2,1)}, bf16[4,256,128]{2,1,0:T(8,128)(2,1)}, f32[2,32,63]{2,1,0:T(8,128)}, f32[128,128]{1,0:T(8,128)}, f32[27,2,128]{2,1,0:T(2,128)}) custom-call(bf16[4,256,128]{2,1,0:T(8,128)(2,1)} %get-tuple-element.15.refs_0_, bf16[4,256,128]{2,1,0:T(8,128)(2,1)} %get-tuple-element.16.refs_1_, ...), custom_call_target="tpu_custom_call" | custom-call | tf_op jit(solution)/shard_map/hand_on/pallas_call | solution.py:563

commit v2 on v1

--- a/solution.py
+++ b/solution.py
@@ -65,6 +65,7 @@
     got_w3,
     weights,
     inverse,
+    inverse2,
     part_p,
     got_p,
     local_sem,
@@ -105,9 +106,8 @@
         at = lax.rem(depth + t, 8)
         return at, device(at // 4, row, col, core, lax.rem(at, 4))
 
-    def along_dp(t):
-        at = lax.rem(quarter + t, 4)
-        return at, device(half, row, col, core, at)
+    def along_dp(t, which):
+        return device(half, row, col, which, lax.rem(quarter + t, 4))
 
     def sixteen(at):
         return pl.ds(pl.multiple_of(at * 16, 16), 16)
@@ -141,6 +141,7 @@
     partners = [sibling, far]
     partners += [in_plane(t)[2] for t in range(1, 16)]
     partners += [along_z(t)[1] for t in range(1, 8)]
+    partners += [along_dp(t, other) for t in range(1, 4)]
     barrier = pltpu.get_barrier_semaphore()
     for partner in partners:
         pl.semaphore_signal(
@@ -287,6 +288,8 @@
     pinv_in.wait()
     for o in range(27):
         inverse[2 * o : 2 * o + 2, 0:3456] = pinv[o]
+    inverse2[core] = inverse[:, pl.ds(pl.multiple_of(quarter * 896, 128), 896)]
+    rows_in = send(inverse2.at[core], inverse2.at[core], sibling)
 
     before.wait_recv()
     place_a(halo_a[0], 0)
@@ -318,20 +321,32 @@
             prod_l[1, s] = both[128:256]
         return swap_l(first, last)
 
-    lc = [lag_block(0, 12)]
-
-    for copy in wc:
-        copy.wait_recv()
-    out_w1[...] = (prod_w[:, :, :, mine, :] + got_wc[...]).astype(BF16)
     w1 = []
-    for t in range(1, 16):
-        at_y, at_x, to = in_plane(t)
-        w1.append(send(out_w1.at[:, :, at_y, sixteen(at_x), :], got_w1.at[t - 1], to))
-
-    lc.append(lag_block(12, 25))
-    for copy in lc:
-        copy.wait_recv()
-    l1 += spread_l(0, 25)
+
+    def spread_w(first, last):
+        for copy in wc[first:last]:
+            copy.wait_recv()
+        out_w1[first:last] = (prod_w[first:last, :, :, mine, :] + got_wc[first:last]).astype(BF16)
+        for t in range(1, 16):
+            at_y, at_x, to = in_plane(t)
+            w1.append(
+                send(
+                    out_w1.at[first:last, :, at_y, sixteen(at_x), :],
+                    got_w1.at[t - 1, first:last],
+                    to,
+                )
+            )
+
+    spread_w(0, 2)
+    lc = [lag_block(0, 6)]
+    spread_w(2, 4)
+    lc.append(lag_block(6, 13))
+    lc.append(lag_block(13, 25))
+    lc[0].wait_recv()
+    lc[1].wait_recv()
+    l1 += spread_l(0, 13)
+    lc[2].wait_recv()
+    l1 += spread_l(13, 25)
 
     for z in range(4):
         place_s(slope[z], z + 1)
@@ -430,17 +445,24 @@
 
     for copy in g1:
         copy.wait_recv()
-    g3 = send(weights.at[:, :, mine, :], weights.at[:, :, mine, :], sibling)
-    g3.wait_recv()
-    cut = pl.ds(pl.multiple_of(quarter * 896, 128), 896)
-    gathered = jnp.concatenate([weights[b // 4, b % 4] for b in range(7)], axis=1)
-    part_p[...] = lax.dot_general(
-        inverse[:, cut], gathered, NT, preferred_element_type=F32, precision=HIGHEST
+    own_in = send(weights.at[1, 3, mine, :], weights.at[1, 3, mine, :], sibling)
+    rows_in.wait_recv()
+    gathered = jnp.concatenate([weights[b // 4, b % 4, mine, :] for b in range(7)], axis=1)
+    both_p = lax.dot_general(
+        inverse2[...].reshape(112, 896),
+        gathered,
+        NT,
+        preferred_element_type=F32,
+        precision=HIGHEST,
     )
-    got_p[quarter] = part_p[...]
-    pp = []
-    for t in range(1, 4):
-        pp.append(send(part_p, got_p.at[quarter], along_dp(t)[1]))
+    part_p[0] = both_p[0:56]
+    part_p[1] = both_p[56:112]
+    got_p[quarter, core] = part_p[core]
+    pp = [send(part_p.at[other], got_p.at[quarter, core], sibling)]
+    for t in (3, 1, 2):
+        for which in (core, other):
+            pp.append(send(part_p.at[which], got_p.at[quarter, core], along_dp(t, which)))
+    own_in.wait_recv()
     output_factor[...] = weights[1, 3] * (1.0 / TOTAL)
 
     for copy in l3:
@@ -462,10 +484,16 @@
     oinv_in.wait()
     for copy in pp:
         copy.wait_recv()
-    product = got_p[0] + got_p[1] + got_p[2] + got_p[3]
-    product = jnp.dot(
-        product, oinv[...], preferred_element_type=F32, precision=HIGHEST
-    ) * (1.0 / TOTAL)
+    product = jnp.zeros((56, 128), F32)
+    for which in range(2):
+        piece = got_p[0, which] + got_p[1, which] + got_p[2, which] + got_p[3, which]
+        product += jnp.dot(
+            piece,
+            oinv[64 * which : 64 * which + 64, :],
+            preferred_element_type=F32,
+            precision=HIGHEST,
+        )
+    product = product * (1.0 / TOTAL)
     for o in range(27):
         precond[o] = product[2 * o : 2 * o + 2]
 
@@ -528,8 +556,9 @@
         ((8, 2, 16, 128), F32),
         ((2, 4, 128, 128), F32),
         ((56, 3584), F32),
-        ((56, 128), F32),
-        ((4, 56, 128), F32),
+        ((2, 56, 896), F32),
+        ((2, 56, 64), F32),
+        ((4, 2, 56, 64), F32),
     ]
     shapes = (
         jax.ShapeDtypeStruct((4, 256, 128), BF16),
@@ -546,8 +575,8 @@
         scratch_shapes=[pltpu.VMEM(shape, dtype) for shape, dtype in scratch]
         + [
             pltpu.SemaphoreType.DMA((8,)),
-            pltpu.SemaphoreType.DMA((96,)),
-            pltpu.SemaphoreType.DMA((96,)),
+            pltpu.SemaphoreType.DMA((128,)),
+            pltpu.SemaphoreType.DMA((128,)),
         ],
         compiler_params=pltpu.CompilerParams(
             collective_id=0, has_side_effects=True, vmem_limit_bytes=60 * 1024 * 1024

time: 57 us -> 57.7 us (1.012)
  Pallas kernels: 56.1 us -> 56.8 us
    pallas_call x1, Pallas kernels: 54.2 us -> 54.9 us  [per_device(): pl.pallas_call(step_kernel, out_shape=shapes, in_specs=[hbm] * 5, out_spe...]
where the time goes in v2:
time: 57.7 us; the launch traced here: 57.6 us
  Pallas kernels  56.8 us (98%)
  between operations  0.8 us (1%)
    pallas_call x1, Pallas kernels, per_device(): pl.pallas_call(step_kernel, out_shape=shapes, in_specs=[hbm] * 5, out_spe...  54.9 us
    pallas_call x1, Pallas kernels, per_device(): pl.pallas_call(hand_on, out_shape=shapes, in_specs=[hbm] * 5, out_specs=[...  1.85 us

profile of v2, /device:TPU:1, one launch (start us, length us, event | category | flops | bytes accessed | tf_op | source)
XLA Modules:
  0.0 57.6 jit_solution(18200262216389020665)
XLA Ops:
  0.6 54.9 %step_kernel.1 = (bf16[4,256,128]{2,1,0:T(8,128)(2,1)}, bf16[4,256,128]{2,1,0:T(8,128)(2,1)}, f32[2,32,63]{2,1,0:T(8,128)}, f32[128,128]{1,0:T(8,128)}, f32[27,2,128]{2,1,0:T(2,128)}) custom-call(bf16[4,256,128]{2,1,0:T(8,128)(2,1)} %bitcast.5, bf16[4,256,128]{2,1,0:T(8,128)(2,1)} %bitcast.6, bf16[27,128,128]{2,1,0:T(8,128)(2,1)} %kw_hbm.1, ...), custom_call_target="tpu_custom_call" | custom-call | tf_op jit(solution)/shard_map/step_kernel/pallas_call | solution.py:570
  55.6 1.9 %hand_on.1 = (bf16[4,256,128]{2,1,0:T(8,128)(2,1)}, bf16[4,256,128]{2,1,0:T(8,128)(2,1)}, f32[2,32,63]{2,1,0:T(8,128)}, f32[128,128]{1,0:T(8,128)}, f32[27,2,128]{2,1,0:T(2,128)}) custom-call(bf16[4,256,128]{2,1,0:T(8,128)(2,1)} %get-tuple-element.15.refs_0_, bf16[4,256,128]{2,1,0:T(8,128)(2,1)} %get-tuple-element.16.refs_1_, ...), custom_call_target="tpu_custom_call" | custom-call | tf_op jit(solution)/shard_map/hand_on/pallas_call | solution.py:592

commit v3 on v2

--- a/solution.py
+++ b/solution.py
@@ -48,6 +48,7 @@
     left,
     left12,
     slope_t,
+    begun,
     prod_l,
     got_lc,
     out_l1,
@@ -182,6 +183,8 @@
             ext_a[dx + 2, at, 32:288, :] = moved
             ext_a[dx + 2, at, 0:32, :] = moved[224:256]
             ext_a[dx + 2, at, 288:320, :] = moved[0:32]
+
+    def turn_a(plane, at):
         for part in range(2):
             left[part, :, at * 256 : (at + 1) * 256] = turned(orders[part], plane)
 
@@ -205,12 +208,13 @@
 
     prod_l[1, 31] = jnp.zeros((128, 128), F32)
     prod_w[3, 1, 2] = jnp.zeros((128, 128), F32)
-    inverse[:, 3456:3584] = jnp.zeros((56, 128), F32)
-    inverse[48:56, :] = jnp.zeros((8, 3584), F32)
+    inverse[:, 3456:3584] = jnp.zeros((64, 128), F32)
+    inverse[48:64, :] = jnp.zeros((16, 3584), F32)
 
     act_in.wait()
     for z in range(4):
         place_a(act[z], z + 1)
+        turn_a(act[z], z + 1)
     for k in range(13):
         m = k + 62
         part, slot = (0, 25 + k) if k < 7 else (1, 18 + k)
@@ -221,20 +225,27 @@
     kw_in.wait()
     up_in.wait()
 
-    def forward(z):
+    def taps_sum(z, depths):
         taps = []
-        for o in range(27):
-            dz, dy, dx = tap_shift(o)
-            taps.append(ext_a[dx + 2, z + 1 + dz, (2 + dy) * 16 : (2 + dy) * 16 + 256, :])
-        pre = dot(jnp.concatenate(taps, axis=1), kw[...].reshape(27 * 128, 128))
+        for dz in depths:
+            for o in range(9):
+                dy, dx = o // 3 - 1, o % 3 - 1
+                first = (2 + dy) * 16
+                taps.append(ext_a[dx + 2, z + 1 + dz, first : first + 256, :])
+        matrix = kw[9 * depths[0] + 9 : 9 * depths[-1] + 18].reshape(len(taps) * 128, 128)
+        return dot(jnp.concatenate(taps, axis=1), matrix)
+
+    def forward(z, pre):
         logistic = jax.nn.sigmoid(pre)
         activated[z] = (pre * logistic).astype(BF16)
         sloped = (up[z].astype(F32) * logistic * (1.0 + pre * (1.0 - logistic))).astype(BF16)
         slope[z] = sloped
         slope_t[:, z * 256 : (z + 1) * 256] = turned(unit, sloped)
 
-    forward(1)
-    forward(2)
+    forward(1, taps_sum(1, (-1, 0, 1)))
+    forward(2, taps_sum(2, (-1, 0, 1)))
+    begun[0] = taps_sum(0, (0, 1))
+    begun[1] = taps_sum(3, (-1, 0))
 
     pl.semaphore_wait(barrier, len(partners))
     before = send(act.at[3], halo_a.at[0], following)
@@ -295,8 +306,8 @@
     place_a(halo_a[0], 0)
     after.wait_recv()
     place_a(halo_a[1], 5)
-    forward(3)
-    forward(0)
+    forward(3, begun[1] + taps_sum(3, (1,)))
+    forward(0, begun[0] + taps_sum(0, (-1,)))
     before_s = send(slope.at[3], halo_s.at[0], following)
     after_s = send(slope.at[0], halo_s.at[1], preceding)
     activated_out = move(activated, activated_hbm)
@@ -310,6 +321,7 @@
             prod_w[d, b // 4, b % 4] += dot(outer_t, ends_a(dz, dy, dx))
         wc.append(send(prod_w.at[d, :, :, theirs, :], got_wc.at[d], sibling))
 
+    turn_a(halo_a[0], 0)
     left12[0:128, :] = left[0, :, 256:1280]
     left12[128:256, :] = left[1, :, 0:1024]
     pairs = [(dy, dx) for dy in range(-2, 3) for dx in range(-2, 3)]
@@ -448,15 +460,17 @@
     own_in = send(weights.at[1, 3, mine, :], weights.at[1, 3, mine, :], sibling)
     rows_in.wait_recv()
     gathered = jnp.concatenate([weights[b // 4, b % 4, mine, :] for b in range(7)], axis=1)
-    both_p = lax.dot_general(
-        inverse2[...].reshape(112, 896),
-        gathered,
-        NT,
-        preferred_element_type=F32,
-        precision=HIGHEST,
-    )
-    part_p[0] = both_p[0:56]
-    part_p[1] = both_p[56:112]
+    blank = jnp.zeros((64, 896), F32)
+    packed_p = jnp.zeros((64, 128), F32)
+    for n in range(2):
+        packed_p += lax.dot_general(
+            inverse2[:, 32 * n : 32 * n + 32, :].reshape(64, 896),
+            jnp.concatenate([gathered, blank] if n == 0 else [blank, gathered], axis=0),
+            NT,
+            preferred_element_type=F32,
+            precision=HIGHEST,
+        )
+    part_p[...] = packed_p.reshape(2, 32, 128)
     got_p[quarter, core] = part_p[core]
     pp = [send(part_p.at[other], got_p.at[quarter, core], sibling)]
     for t in (3, 1, 2):
@@ -484,16 +498,19 @@
     oinv_in.wait()
     for copy in pp:
         copy.wait_recv()
-    product = jnp.zeros((56, 128), F32)
+    products = [jnp.zeros((32, 128), F32), jnp.zeros((32, 128), F32)]
+    empty = jnp.zeros((64, 128), F32)
     for which in range(2):
         piece = got_p[0, which] + got_p[1, which] + got_p[2, which] + got_p[3, which]
-        product += jnp.dot(
-            piece,
-            oinv[64 * which : 64 * which + 64, :],
-            preferred_element_type=F32,
-            precision=HIGHEST,
-        )
-    product = product * (1.0 / TOTAL)
+        factor = oinv[64 * which : 64 * which + 64, :]
+        for n in range(2):
+            products[n] += jnp.dot(
+                piece,
+                jnp.concatenate([factor, empty] if n == 0 else [empty, factor], axis=0),
+                preferred_element_type=F32,
+                precision=HIGHEST,
+            )
+    product = jnp.concatenate(products, axis=0) * (1.0 / TOTAL)
     for o in range(27):
         precond[o] = product[2 * o : 2 * o + 2]
 
@@ -539,6 +556,7 @@
         ((2, 128, 1536), BF16),
         ((256, 1024), BF16),
         ((128, 1024), BF16),
+        ((2, 256, 128), F32),
         ((2, 32, 128, 128), F32),
         ((2, 32, 64, 128), F32),
         ((2, 32, 64, 128), BF16),
@@ -555,10 +573,10 @@
         ((4, 2, 16, 128), F32),
         ((8, 2, 16, 128), F32),
         ((2, 4, 128, 128), F32),
-        ((56, 3584), F32),
-        ((2, 56, 896), F32),
-        ((2, 56, 64), F32),
-        ((4, 2, 56, 64), F32),
+        ((64, 3584), F32),
+        ((2, 64, 896), F32),
+        ((2, 32, 128), F32),
+        ((4, 2, 32, 128), F32),
     ]
     shapes = (
         jax.ShapeDtypeStruct((4, 256, 128), BF16),

time: 57.7 us -> 54.8 us (0.950)
  Pallas kernels: 56.8 us -> 53.9 us
    pallas_call x1, Pallas kernels: 54.9 us -> 52.1 us  [per_device(): pl.pallas_call(step_kernel, out_shape=shapes, in_specs=[hbm] * 5, out_spe...]
where the time goes in v3:
time: 54.8 us; the launch traced here: 54.7 us
  Pallas kernels  53.9 us (98%)
  between operations  0.8 us (1%)
    pallas_call x1, Pallas kernels, per_device(): pl.pallas_call(step_kernel, out_shape=shapes, in_specs=[hbm] * 5, out_spe...  52.1 us
    pallas_call x1, Pallas kernels, per_device(): pl.pallas_call(hand_on, out_shape=shapes, in_specs=[hbm] * 5, out_specs=[...  1.85 us

profile of v3, /device:TPU:1, one launch (start us, length us, event | category | flops | bytes accessed | tf_op | source)
XLA Modules:
  0.0 54.7 jit_solution(8458997692439687422)
XLA Ops:
  0.6 52.1 %step_kernel.1 = (bf16[4,256,128]{2,1,0:T(8,128)(2,1)}, bf16[4,256,128]{2,1,0:T(8,128)(2,1)}, f32[2,32,63]{2,1,0:T(8,128)}, f32[128,128]{1,0:T(8,128)}, f32[27,2,128]{2,1,0:T(2,128)}) custom-call(bf16[4,256,128]{2,1,0:T(8,128)(2,1)} %bitcast.5, bf16[4,256,128]{2,1,0:T(8,128)(2,1)} %bitcast.6, bf16[27,128,128]{2,1,0:T(8,128)(2,1)} %kw_hbm.1, ...), custom_call_target="tpu_custom_call" | custom-call | tf_op jit(solution)/shard_map/step_kernel/pallas_call | solution.py:588
  52.7 1.9 %hand_on.1 = (bf16[4,256,128]{2,1,0:T(8,128)(2,1)}, bf16[4,256,128]{2,1,0:T(8,128)(2,1)}, f32[2,32,63]{2,1,0:T(8,128)}, f32[128,128]{1,0:T(8,128)}, f32[27,2,128]{2,1,0:T(2,128)}) custom-call(bf16[4,256,128]{2,1,0:T(8,128)(2,1)} %get-tuple-element.15.refs_0_, bf16[4,256,128]{2,1,0:T(8,128)(2,1)} %get-tuple-element.16.refs_1_, ...), custom_call_target="tpu_custom_call" | custom-call | tf_op jit(solution)/shard_map/hand_on/pallas_call | solution.py:610

commit v4 on v3

--- a/solution.py
+++ b/solution.py
@@ -10,6 +10,8 @@
 F32 = jnp.float32
 BF16 = jnp.bfloat16
 TOTAL = 262144.0
+PLANE = (10, 6, 9, 11, 14, 5, 7, 13, 15, 2, 8, 1, 3, 4, 12)
+RING = (4, 3, 5, 2, 6, 1, 7)
 NT = (((1,), (1,)), ((), ()))
 HIGHEST = lax.Precision.HIGHEST
 
@@ -139,10 +141,11 @@
         copy.start()
         return copy
 
-    partners = [sibling, far]
-    partners += [in_plane(t)[2] for t in range(1, 16)]
-    partners += [along_z(t)[1] for t in range(1, 8)]
-    partners += [along_dp(t, other) for t in range(1, 4)]
+    partners = [far]
+    partners += [along_z(t)[1] for t in RING]
+    partners += [in_plane(t)[2] for t in PLANE]
+    partners += [along_dp(t, other) for t in (3, 1, 2)]
+    partners += [sibling]
     barrier = pltpu.get_barrier_semaphore()
     for partner in partners:
         pl.semaphore_signal(
@@ -222,8 +225,9 @@
             left[part, :, 256:1280], rows_a(1, m // 5 % 5 - 2, m % 5 - 2)
         )
 
-    kw_in.wait()
-    up_in.wait()
+    pl.semaphore_wait(barrier, len(partners))
+    before = send(act.at[3], halo_a.at[0], following)
+    after = send(act.at[0], halo_a.at[1], preceding)
 
     def taps_sum(z, depths):
         taps = []
@@ -242,15 +246,6 @@
         slope[z] = sloped
         slope_t[:, z * 256 : (z + 1) * 256] = turned(unit, sloped)
 
-    forward(1, taps_sum(1, (-1, 0, 1)))
-    forward(2, taps_sum(2, (-1, 0, 1)))
-    begun[0] = taps_sum(0, (0, 1))
-    begun[1] = taps_sum(3, (-1, 0))
-
-    pl.semaphore_wait(barrier, len(partners))
-    before = send(act.at[3], halo_a.at[0], following)
-    after = send(act.at[0], halo_a.at[1], preceding)
-
     theirs = pl.ds(pl.multiple_of(other * 64, 64), 64)
     mine = pl.ds(pl.multiple_of(core * 64, 64), 64)
     firsts = (col, row)
@@ -269,7 +264,7 @@
             out_l1[part, first:last] = (
                 prod_l[part, first:last, mine, :] + got_lc[part, first:last]
             ).astype(BF16)
-            for t in range(1, 4):
+            for t in (2, 1, 3):
                 at, to = first_axis[part](t)
                 copies.append(
                     send(
@@ -281,6 +276,12 @@
         return copies
 
     early_c = swap_l(25, 32)
+    kw_in.wait()
+    up_in.wait()
+    forward(1, taps_sum(1, (-1, 0, 1)))
+    forward(2, taps_sum(2, (-1, 0, 1)))
+    begun[0] = taps_sum(0, (0, 1))
+    begun[1] = taps_sum(3, (-1, 0))
 
     def blocks(d):
         for b in range(7):
@@ -339,7 +340,7 @@
         for copy in wc[first:last]:
             copy.wait_recv()
         out_w1[first:last] = (prod_w[first:last, :, :, mine, :] + got_wc[first:last]).astype(BF16)
-        for t in range(1, 16):
+        for t in PLANE:
             at_y, at_x, to = in_plane(t)
             w1.append(
                 send(
@@ -390,7 +391,7 @@
     out_w3[...] = total_w
     got_w3[depth] = out_w3[quarter]
     w3 = []
-    for t in range(1, 8):
+    for t in RING:
         at, to = along_z(t)
         w3.append(send(out_w3.at[lax.rem(at, 4)], got_w3.at[depth], to))
 
@@ -408,11 +409,11 @@
         sum_l1[part] = total.reshape(512, 128)
         for b in range(4):
             for n in range(4):
-                for g in range(4):
-                    out_l2[part, b, n, 8 * g : 8 * g + 8, :] = sum_l1[
-                        part, pl.ds(4 * b + n + 128 * g, 8, stride=16), :
-                    ]
-        for t in range(1, 4):
+                groups = [
+                    sum_l1[part, pl.ds(4 * b + n + 128 * g, 8, stride=16), :] for g in range(4)
+                ]
+                out_l2[part, b, n] = jnp.concatenate(groups, axis=0).astype(BF16)
+        for t in (2, 1, 3):
             at, to = second_axis[part](t)
             l2.append(send(out_l2.at[part, at], got_l2.at[part, t - 1], to))
 
@@ -425,7 +426,7 @@
         reduced = reduced + got_w3[z]
     weights[:, row, tall, :] = reduced
     g1 = []
-    for t in range(1, 16):
+    for t in PLANE:
         piece = weights.at[:, row, tall, :]
         g1.append(send(piece, piece, in_plane(t)[2]))
 
@@ -437,9 +438,9 @@
     group = c[0:32] // 32
     totals = []
     for part in range(2):
-        total = out_l2[part, seconds[part]]
+        total = out_l2[part, seconds[part]].astype(F32)
         for t in range(3):
-            total = total + got_l2[part, t]
+            total = total + got_l2[part, t].astype(F32)
         totals.append(total)
     for h in range(2):
         groups = [totals[part][2 * h + i] for part in range(2) for i in range(2)]
@@ -451,7 +452,7 @@
                 packed = jnp.where(group == j, piece, packed)
             out_l3[4 * h + q] = packed
     l3 = []
-    for t in range(1, 8):
+    for t in RING:
         at, to = along_z(t)
         l3.append(send(out_l3.at[at], got_l3.at[t - 1], to))
 
@@ -562,8 +563,8 @@
         ((2, 32, 64, 128), BF16),
         ((2, 3, 32, 16, 128), BF16),
         ((2, 512, 128), F32),
-        ((2, 4, 4, 32, 128), F32),
-        ((2, 3, 4, 32, 128), F32),
+        ((2, 4, 4, 32, 128), BF16),
+        ((2, 3, 4, 32, 128), BF16),
         ((8, 32, 128), F32),
         ((7, 32, 128), F32),
         ((4, 2, 4, 128, 128), F32),

time: 54.8 us -> 53 us (0.967)
  Pallas kernels: 53.9 us -> 52.1 us
    pallas_call x1, Pallas kernels: 52.1 us -> 50.2 us  [per_device(): pl.pallas_call(step_kernel, out_shape=shapes, in_specs=[hbm] * 5, out_spe...]
where the time goes in v4:
time: 53 us; the launch traced here: 52.9 us
  Pallas kernels  52.1 us (98%)
  between operations  0.8 us (2%)
    pallas_call x1, Pallas kernels, per_device(): pl.pallas_call(step_kernel, out_shape=shapes, in_specs=[hbm] * 5, out_spe...  50.2 us
    pallas_call x1, Pallas kernels, per_device(): pl.pallas_call(hand_on, out_shape=shapes, in_specs=[hbm] * 5, out_specs=[...  1.85 us

profile of v4, /device:TPU:1, one launch (start us, length us, event | category | flops | bytes accessed | tf_op | source)
XLA Modules:
  0.0 52.9 jit_solution(822545306485909215)
XLA Ops:
  0.6 50.2 %step_kernel.1 = (bf16[4,256,128]{2,1,0:T(8,128)(2,1)}, bf16[4,256,128]{2,1,0:T(8,128)(2,1)}, f32[2,32,63]{2,1,0:T(8,128)}, f32[128,128]{1,0:T(8,128)}, f32[27,2,128]{2,1,0:T(2,128)}) custom-call(bf16[4,256,128]{2,1,0:T(8,128)(2,1)} %bitcast.5, bf16[4,256,128]{2,1,0:T(8,128)(2,1)} %bitcast.6, bf16[27,128,128]{2,1,0:T(8,128)(2,1)} %kw_hbm.1, ...), custom_call_target="tpu_custom_call" | custom-call | tf_op jit(solution)/shard_map/step_kernel/pallas_call | solution.py:589
  50.9 1.9 %hand_on.1 = (bf16[4,256,128]{2,1,0:T(8,128)(2,1)}, bf16[4,256,128]{2,1,0:T(8,128)(2,1)}, f32[2,32,63]{2,1,0:T(8,128)}, f32[128,128]{1,0:T(8,128)}, f32[27,2,128]{2,1,0:T(2,128)}) custom-call(bf16[4,256,128]{2,1,0:T(8,128)(2,1)} %get-tuple-element.15.refs_0_, bf16[4,256,128]{2,1,0:T(8,128)(2,1)} %get-tuple-element.16.refs_1_, ...), custom_call_target="tpu_custom_call" | custom-call | tf_op jit(solution)/shard_map/hand_on/pallas_call | solution.py:611

commit v5 on v4

--- a/solution.py
+++ b/solution.py
@@ -117,7 +117,6 @@
 
     count = [0, 0]
     sent = []
-    moved_out = []
 
     def send(src, dst, to):
         n = count[0]
@@ -134,6 +133,13 @@
         sent.append(copy)
         return copy
 
+    settled = [0]
+
+    def settle(upto):
+        for copy in sent[settled[0] : upto]:
+            copy.wait_send()
+        settled[0] = upto
+
     def move(src, dst):
         n = count[1]
         count[1] += 1
@@ -177,9 +183,9 @@
     def turned(order, plane):
         return lax.dot_general(order, plane, NT, preferred_element_type=F32).astype(BF16)
 
-    def place_a(plane, at):
+    def place_a(plane, at, shifts):
         wide = plane.astype(F32).reshape(16, 16, 128)
-        for dx in range(-2, 3):
+        for dx in shifts:
             moved = plane
             if dx:
                 moved = pltpu.roll(wide, (-dx) % 16, 1).reshape(256, 128).astype(BF16)
@@ -216,7 +222,7 @@
 
     act_in.wait()
     for z in range(4):
-        place_a(act[z], z + 1)
+        place_a(act[z], z + 1, (-2, -1, 0, 1, 2))
         turn_a(act[z], z + 1)
     for k in range(13):
         m = k + 62
@@ -304,9 +310,9 @@
     rows_in = send(inverse2.at[core], inverse2.at[core], sibling)
 
     before.wait_recv()
-    place_a(halo_a[0], 0)
+    place_a(halo_a[0], 0, (-1, 0, 1))
     after.wait_recv()
-    place_a(halo_a[1], 5)
+    place_a(halo_a[1], 5, (-1, 0, 1))
     forward(3, begun[1] + taps_sum(3, (1,)))
     forward(0, begun[0] + taps_sum(0, (-1,)))
     before_s = send(slope.at[3], halo_s.at[0], following)
@@ -323,6 +329,7 @@
         wc.append(send(prod_w.at[d, :, :, theirs, :], got_wc.at[d], sibling))
 
     turn_a(halo_a[0], 0)
+    place_a(halo_a[1], 5, (-2, 2))
     left12[0:128, :] = left[0, :, 256:1280]
     left12[128:256, :] = left[1, :, 0:1024]
     pairs = [(dy, dx) for dy in range(-2, 3) for dx in range(-2, 3)]
@@ -355,6 +362,7 @@
     spread_w(2, 4)
     lc.append(lag_block(6, 13))
     lc.append(lag_block(13, 25))
+    spread_from = len(sent)
     lc[0].wait_recv()
     lc[1].wait_recv()
     l1 += spread_l(0, 13)
@@ -382,14 +390,18 @@
 
     back(0)
 
-    for copy in w1:
-        copy.wait_recv()
+    settle(spread_from)
     tall = sixteen(core * 4 + col)
-    total_w = prod_w[:, :, row, tall, :] + got_wc[:, :, row, sixteen(col), :]
-    for t in range(15):
-        total_w = total_w + got_w1[t].astype(F32)
-    out_w3[...] = total_w
+    for n in range(2):
+        for copy in w1[15 * n : 15 * n + 15]:
+            copy.wait_recv()
+        two = slice(2 * n, 2 * n + 2)
+        total_w = prod_w[two, :, row, tall, :] + got_wc[two, :, row, sixteen(col), :]
+        for t in range(15):
+            total_w = total_w + got_w1[t, two].astype(F32)
+        out_w3[two] = total_w
     got_w3[depth] = out_w3[quarter]
+    z_from = len(sent)
     w3 = []
     for t in RING:
         at, to = along_z(t)
@@ -419,12 +431,14 @@
 
     back(2)
 
+    settle(z_from)
     for copy in w3:
         copy.wait_recv()
     reduced = got_w3[0]
     for z in range(1, 8):
         reduced = reduced + got_w3[z]
     weights[:, row, tall, :] = reduced
+    gather_from = len(sent)
     g1 = []
     for t in PLANE:
         piece = weights.at[:, row, tall, :]
@@ -456,6 +470,7 @@
         at, to = along_z(t)
         l3.append(send(out_l3.at[at], got_l3.at[t - 1], to))
 
+    settle(gather_from)
     for copy in g1:
         copy.wait_recv()
     own_in = send(weights.at[1, 3, mine, :], weights.at[1, 3, mine, :], sibling)
@@ -473,6 +488,7 @@
         )
     part_p[...] = packed_p.reshape(2, 32, 128)
     got_p[quarter, core] = part_p[core]
+    last_from = len(sent)
     pp = [send(part_p.at[other], got_p.at[quarter, core], sibling)]
     for t in (3, 1, 2):
         for which in (core, other):
@@ -497,6 +513,7 @@
         patch_factor[i] = piece[:, 0:63]
 
     oinv_in.wait()
+    settle(last_from)
     for copy in pp:
         copy.wait_recv()
     products = [jnp.zeros((32, 128), F32), jnp.zeros((32, 128), F32)]
@@ -517,8 +534,7 @@
 
     activated_out.wait()
     input_grad_out.wait()
-    for copy in sent:
-        copy.wait_send()
+    settle(len(sent))
 
 
 def hand_on(*refs):

time: 53 us -> 52.8 us (level)
  no operation moved by 1% of the time
where the time goes in v5:
time: 52.8 us; the launch traced here: 52.7 us
  Pallas kernels  51.9 us (98%)
  between operations  0.8 us (2%)
    pallas_call x1, Pallas kernels, per_device(): pl.pallas_call(step_kernel, out_shape=shapes, in_specs=[hbm] * 5, out_spe...  50 us
    pallas_call x1, Pallas kernels, per_device(): pl.pallas_call(hand_on, out_shape=shapes, in_specs=[hbm] * 5, out_specs=[...  1.85 us

profile of v5, /device:TPU:1, one launch (start us, length us, event | category | flops | bytes accessed | tf_op | source)
XLA Modules:
  0.0 52.7 jit_solution(14661009668616636443)
XLA Ops:
  0.6 50.0 %step_kernel.1 = (bf16[4,256,128]{2,1,0:T(8,128)(2,1)}, bf16[4,256,128]{2,1,0:T(8,128)(2,1)}, f32[2,32,63]{2,1,0:T(8,128)}, f32[128,128]{1,0:T(8,128)}, f32[27,2,128]{2,1,0:T(2,128)}) custom-call(bf16[4,256,128]{2,1,0:T(8,128)(2,1)} %bitcast.5, bf16[4,256,128]{2,1,0:T(8,128)(2,1)} %bitcast.6, bf16[27,128,128]{2,1,0:T(8,128)(2,1)} %kw_hbm.1, ...), custom_call_target="tpu_custom_call" | custom-call | tf_op jit(solution)/shard_map/step_kernel/pallas_call | solution.py:605
  50.7 1.9 %hand_on.1 = (bf16[4,256,128]{2,1,0:T(8,128)(2,1)}, bf16[4,256,128]{2,1,0:T(8,128)(2,1)}, f32[2,32,63]{2,1,0:T(8,128)}, f32[128,128]{1,0:T(8,128)}, f32[27,2,128]{2,1,0:T(2,128)}) custom-call(bf16[4,256,128]{2,1,0:T(8,128)(2,1)} %get-tuple-element.15.refs_0_, bf16[4,256,128]{2,1,0:T(8,128)(2,1)} %get-tuple-element.16.refs_1_, ...), custom_call_target="tpu_custom_call" | custom-call | tf_op jit(solution)/shard_map/hand_on/pallas_call | solution.py:627

commit v6 on v5

--- a/solution.py
+++ b/solution.py
@@ -69,6 +69,7 @@
     weights,
     inverse,
     inverse2,
+    parts2,
     part_p,
     got_p,
     local_sem,
@@ -324,8 +325,10 @@
     wc = []
     for d in range(4):
         prod_w[d, 1, 3] = own
-        for b, (dz, dy, dx) in blocks(d):
-            prod_w[d, b // 4, b % 4] += dot(outer_t, ends_a(dz, dy, dx))
+        ends = jnp.concatenate([ends_a(*shift) for _, shift in blocks(d)], axis=1)
+        wide = dot(outer_t, ends)
+        for b, _ in blocks(d):
+            prod_w[d, b // 4, b % 4] += wide[:, 128 * b : 128 * b + 128]
         wc.append(send(prod_w.at[d, :, :, theirs, :], got_wc.at[d], sibling))
 
     turn_a(halo_a[0], 0)
@@ -390,6 +393,11 @@
 
     back(0)
 
+    rows_in.wait_recv()
+    both_rows = inverse2[...].reshape(128, 896)
+    rows_high = both_rows.astype(BF16)
+    parts2[0:128, :] = rows_high
+    parts2[128:256, :] = (both_rows - rows_high.astype(F32)).astype(BF16)
     settle(spread_from)
     tall = sixteen(core * 4 + col)
     for n in range(2):
@@ -474,19 +482,19 @@
     for copy in g1:
         copy.wait_recv()
     own_in = send(weights.at[1, 3, mine, :], weights.at[1, 3, mine, :], sibling)
-    rows_in.wait_recv()
     gathered = jnp.concatenate([weights[b // 4, b % 4, mine, :] for b in range(7)], axis=1)
-    blank = jnp.zeros((64, 896), F32)
-    packed_p = jnp.zeros((64, 128), F32)
-    for n in range(2):
-        packed_p += lax.dot_general(
-            inverse2[:, 32 * n : 32 * n + 32, :].reshape(64, 896),
-            jnp.concatenate([gathered, blank] if n == 0 else [blank, gathered], axis=0),
-            NT,
-            preferred_element_type=F32,
-            precision=HIGHEST,
+    twice = jnp.concatenate([gathered, gathered], axis=0)
+    twice_high = twice.astype(BF16)
+    twice_low = (twice - twice_high.astype(F32)).astype(BF16)
+    by_high = lax.dot_general(parts2[...], twice_high, NT, preferred_element_type=F32)
+    by_low = lax.dot_general(parts2[0:128, :], twice_low, NT, preferred_element_type=F32)
+    all_p = by_high[0:128] + (by_high[128:256] + by_low)
+    left_half = c[0:32] < 64
+    for which in range(2):
+        base = 64 * which
+        part_p[which] = jnp.where(
+            left_half, all_p[base : base + 32], all_p[base + 32 : base + 64]
         )
-    part_p[...] = packed_p.reshape(2, 32, 128)
     got_p[quarter, core] = part_p[core]
     last_from = len(sent)
     pp = [send(part_p.at[other], got_p.at[quarter, core], sibling)]
@@ -516,19 +524,17 @@
     settle(last_from)
     for copy in pp:
         copy.wait_recv()
-    products = [jnp.zeros((32, 128), F32), jnp.zeros((32, 128), F32)]
-    empty = jnp.zeros((64, 128), F32)
-    for which in range(2):
-        piece = got_p[0, which] + got_p[1, which] + got_p[2, which] + got_p[3, which]
-        factor = oinv[64 * which : 64 * which + 64, :]
-        for n in range(2):
-            products[n] += jnp.dot(
-                piece,
-                jnp.concatenate([factor, empty] if n == 0 else [empty, factor], axis=0),
-                preferred_element_type=F32,
-                precision=HIGHEST,
-            )
-    product = jnp.concatenate(products, axis=0) * (1.0 / TOTAL)
+    zero, one = (got_p[0, n] + got_p[1, n] + got_p[2, n] + got_p[3, n] for n in range(2))
+    product = jnp.concatenate(
+        [
+            jnp.where(left_half, zero, pltpu.roll(one, 64, 1)),
+            jnp.where(left_half, pltpu.roll(zero, 64, 1), one),
+        ],
+        axis=0,
+    )
+    product = jnp.dot(
+        product, oinv[...], preferred_element_type=F32, precision=HIGHEST
+    ) * (1.0 / TOTAL)
     for o in range(27):
         precond[o] = product[2 * o : 2 * o + 2]
 
@@ -592,6 +598,7 @@
         ((2, 4, 128, 128), F32),
         ((64, 3584), F32),
         ((2, 64, 896), F32),
+        ((256, 896), BF16),
         ((2, 32, 128), F32),
         ((4, 2, 32, 128), F32),
     ]

time: 52.8 us -> 52.3 us (level)
  no operation moved by 1% of the time
where the time goes in v6:
time: 52.3 us; the launch traced here: 52.2 us
  Pallas kernels  51.4 us (98%)
  between operations  0.8 us (2%)
    pallas_call x1, Pallas kernels, per_device(): pl.pallas_call(step_kernel, out_shape=shapes, in_specs=[hbm] * 5, out_spe...  49.5 us
    pallas_call x1, Pallas kernels, per_device(): pl.pallas_call(hand_on, out_shape=shapes, in_specs=[hbm] * 5, out_specs=[...  1.85 us

profile of v6, /device:TPU:1, one launch (start us, length us, event | category | flops | bytes accessed | tf_op | source)
XLA Modules:
  0.0 52.2 jit_solution(6009374609250763146)
XLA Ops:
  0.6 49.5 %step_kernel.1 = (bf16[4,256,128]{2,1,0:T(8,128)(2,1)}, bf16[4,256,128]{2,1,0:T(8,128)(2,1)}, f32[2,32,63]{2,1,0:T(8,128)}, f32[128,128]{1,0:T(8,128)}, f32[27,2,128]{2,1,0:T(2,128)}) custom-call(bf16[4,256,128]{2,1,0:T(8,128)(2,1)} %bitcast.5, bf16[4,256,128]{2,1,0:T(8,128)(2,1)} %bitcast.6, bf16[27,128,128]{2,1,0:T(8,128)(2,1)} %kw_hbm.1, ...), custom_call_target="tpu_custom_call" | custom-call | tf_op jit(solution)/shard_map/step_kernel/pallas_call | solution.py:612
  50.2 1.9 %hand_on.1 = (bf16[4,256,128]{2,1,0:T(8,128)(2,1)}, bf16[4,256,128]{2,1,0:T(8,128)(2,1)}, f32[2,32,63]{2,1,0:T(8,128)}, f32[128,128]{1,0:T(8,128)}, f32[27,2,128]{2,1,0:T(2,128)}) custom-call(bf16[4,256,128]{2,1,0:T(8,128)(2,1)} %get-tuple-element.15.refs_0_, bf16[4,256,128]{2,1,0:T(8,128)(2,1)} %get-tuple-element.16.refs_1_, ...), custom_call_target="tpu_custom_call" | custom-call | tf_op jit(solution)/shard_map/hand_on/pallas_call | solution.py:634

commit v7 on v6

--- a/solution.py
+++ b/solution.py
@@ -331,10 +331,6 @@
             prod_w[d, b // 4, b % 4] += wide[:, 128 * b : 128 * b + 128]
         wc.append(send(prod_w.at[d, :, :, theirs, :], got_wc.at[d], sibling))
 
-    turn_a(halo_a[0], 0)
-    place_a(halo_a[1], 5, (-2, 2))
-    left12[0:128, :] = left[0, :, 256:1280]
-    left12[128:256, :] = left[1, :, 0:1024]
     pairs = [(dy, dx) for dy in range(-2, 3) for dx in range(-2, 3)]
 
     def lag_block(first, last):
@@ -361,9 +357,12 @@
             )
 
     spread_w(0, 2)
-    lc = [lag_block(0, 6)]
+    turn_a(halo_a[0], 0)
+    place_a(halo_a[1], 5, (-2, 2))
+    left12[0:128, :] = left[0, :, 256:1280]
+    left12[128:256, :] = left[1, :, 0:1024]
     spread_w(2, 4)
-    lc.append(lag_block(6, 13))
+    lc = [lag_block(0, 6), lag_block(6, 13)]
     lc.append(lag_block(13, 25))
     spread_from = len(sent)
     lc[0].wait_recv()

time: 52.3 us -> 52.9 us (1.011)
  Pallas kernels: 51.4 us -> 52 us
    pallas_call x1, Pallas kernels: 49.5 us -> 50.1 us  [per_device(): pl.pallas_call(step_kernel, out_shape=shapes, in_specs=[hbm] * 5, out_spe...]
where the time goes in v7:
time: 52.9 us; the launch traced here: 52.8 us
  Pallas kernels  52 us (98%)
  between operations  0.8 us (2%)
    pallas_call x1, Pallas kernels, per_device(): pl.pallas_call(step_kernel, out_shape=shapes, in_specs=[hbm] * 5, out_spe...  50.1 us
    pallas_call x1, Pallas kernels, per_device(): pl.pallas_call(hand_on, out_shape=shapes, in_specs=[hbm] * 5, out_specs=[...  1.85 us

profile of v7, /device:TPU:1, one launch (start us, length us, event | category | flops | bytes accessed | tf_op | source)
XLA Modules:
  0.0 52.8 jit_solution(7463706147468528657)
XLA Ops:
  0.6 50.1 %step_kernel.1 = (bf16[4,256,128]{2,1,0:T(8,128)(2,1)}, bf16[4,256,128]{2,1,0:T(8,128)(2,1)}, f32[2,32,63]{2,1,0:T(8,128)}, f32[128,128]{1,0:T(8,128)}, f32[27,2,128]{2,1,0:T(2,128)}) custom-call(bf16[4,256,128]{2,1,0:T(8,128)(2,1)} %bitcast.5, bf16[4,256,128]{2,1,0:T(8,128)(2,1)} %bitcast.6, bf16[27,128,128]{2,1,0:T(8,128)(2,1)} %kw_hbm.1, ...), custom_call_target="tpu_custom_call" | custom-call | tf_op jit(solution)/shard_map/step_kernel/pallas_call | solution.py:611
  50.8 1.9 %hand_on.1 = (bf16[4,256,128]{2,1,0:T(8,128)(2,1)}, bf16[4,256,128]{2,1,0:T(8,128)(2,1)}, f32[2,32,63]{2,1,0:T(8,128)}, f32[128,128]{1,0:T(8,128)}, f32[27,2,128]{2,1,0:T(2,128)}) custom-call(bf16[4,256,128]{2,1,0:T(8,128)(2,1)} %get-tuple-element.15.refs_0_, bf16[4,256,128]{2,1,0:T(8,128)(2,1)} %get-tuple-element.16.refs_1_, ...), custom_call_target="tpu_custom_call" | custom-call | tf_op jit(solution)/shard_map/hand_on/pallas_call | solution.py:633

commit v8 on v6

--- a/solution.py
+++ b/solution.py
@@ -415,8 +415,6 @@
         at, to = along_z(t)
         w3.append(send(out_w3.at[lax.rem(at, 4)], got_w3.at[depth], to))
 
-    back(1)
-
     for copy in l1:
         copy.wait_recv()
     l2 = []
@@ -437,6 +435,7 @@
             at, to = second_axis[part](t)
             l2.append(send(out_l2.at[part, at], got_l2.at[part, t - 1], to))
 
+    back(1)
     back(2)
 
     settle(z_from)
@@ -451,9 +450,6 @@
     for t in PLANE:
         piece = weights.at[:, row, tall, :]
         g1.append(send(piece, piece, in_plane(t)[2]))
-
-    back(3)
-    input_grad_out = move(input_grad, input_grad_hbm)
 
     for copy in l2:
         copy.wait_recv()
@@ -477,6 +473,9 @@
     for t in RING:
         at, to = along_z(t)
         l3.append(send(out_l3.at[at], got_l3.at[t - 1], to))
+
+    back(3)
+    input_grad_out = move(input_grad, input_grad_hbm)
 
     settle(gather_from)
     for copy in g1:

time: 52.3 us -> 52.3 us (level)
  no operation moved by 1% of the time
where the time goes in v8:
time: 52.3 us; the launch traced here: 52.2 us
  Pallas kernels  51.4 us (98%)
  between operations  0.8 us (2%)
    pallas_call x1, Pallas kernels, per_device(): pl.pallas_call(step_kernel, out_shape=shapes, in_specs=[hbm] * 5, out_spe...  49.5 us
    pallas_call x1, Pallas kernels, per_device(): pl.pallas_call(hand_on, out_shape=shapes, in_specs=[hbm] * 5, out_specs=[...  1.85 us

profile of v8, /device:TPU:1, one launch (start us, length us, event | category | flops | bytes accessed | tf_op | source)
XLA Modules:
  0.0 52.2 jit_solution(1843945875011037103)
XLA Ops:
  0.6 49.5 %step_kernel.1 = (bf16[4,256,128]{2,1,0:T(8,128)(2,1)}, bf16[4,256,128]{2,1,0:T(8,128)(2,1)}, f32[2,32,63]{2,1,0:T(8,128)}, f32[128,128]{1,0:T(8,128)}, f32[27,2,128]{2,1,0:T(2,128)}) custom-call(bf16[4,256,128]{2,1,0:T(8,128)(2,1)} %bitcast.5, bf16[4,256,128]{2,1,0:T(8,128)(2,1)} %bitcast.6, bf16[27,128,128]{2,1,0:T(8,128)(2,1)} %kw_hbm.1, ...), custom_call_target="tpu_custom_call" | custom-call | tf_op jit(solution)/shard_map/step_kernel/pallas_call | solution.py:611
  50.2 1.9 %hand_on.1 = (bf16[4,256,128]{2,1,0:T(8,128)(2,1)}, bf16[4,256,128]{2,1,0:T(8,128)(2,1)}, f32[2,32,63]{2,1,0:T(8,128)}, f32[128,128]{1,0:T(8,128)}, f32[27,2,128]{2,1,0:T(2,128)}) custom-call(bf16[4,256,128]{2,1,0:T(8,128)(2,1)} %get-tuple-element.15.refs_0_, bf16[4,256,128]{2,1,0:T(8,128)(2,1)} %get-tuple-element.16.refs_1_, ...), custom_call_target="tpu_custom_call" | custom-call | tf_op jit(solution)/shard_map/hand_on/pallas_call | solution.py:633

commit v9 on v8

--- a/solution.py
+++ b/solution.py
@@ -225,16 +225,16 @@
     for z in range(4):
         place_a(act[z], z + 1, (-2, -1, 0, 1, 2))
         turn_a(act[z], z + 1)
+    pl.semaphore_wait(barrier, len(partners))
+    before = send(act.at[3], halo_a.at[0], following)
+    after = send(act.at[0], halo_a.at[1], preceding)
+
     for k in range(13):
         m = k + 62
         part, slot = (0, 25 + k) if k < 7 else (1, 18 + k)
         prod_l[part, slot] = dot(
             left[part, :, 256:1280], rows_a(1, m // 5 % 5 - 2, m % 5 - 2)
         )
-
-    pl.semaphore_wait(barrier, len(partners))
-    before = send(act.at[3], halo_a.at[0], following)
-    after = send(act.at[0], halo_a.at[1], preceding)
 
     def taps_sum(z, depths):
         taps = []

time: 52.3 us -> 52.3 us (level)
  no operation moved by 1% of the time
where the time goes in v9:
time: 52.3 us; the launch traced here: 52.2 us
  Pallas kernels  51.4 us (98%)
  between operations  0.8 us (2%)
    pallas_call x1, Pallas kernels, per_device(): pl.pallas_call(step_kernel, out_shape=shapes, in_specs=[hbm] * 5, out_spe...  49.5 us
    pallas_call x1, Pallas kernels, per_device(): pl.pallas_call(hand_on, out_shape=shapes, in_specs=[hbm] * 5, out_specs=[...  1.85 us

profile of v9, /device:TPU:1, one launch (start us, length us, event | category | flops | bytes accessed | tf_op | source)
XLA Modules:
  0.0 52.2 jit_solution(17719109161097115941)
XLA Ops:
  0.6 49.5 %step_kernel.1 = (bf16[4,256,128]{2,1,0:T(8,128)(2,1)}, bf16[4,256,128]{2,1,0:T(8,128)(2,1)}, f32[2,32,63]{2,1,0:T(8,128)}, f32[128,128]{1,0:T(8,128)}, f32[27,2,128]{2,1,0:T(2,128)}) custom-call(bf16[4,256,128]{2,1,0:T(8,128)(2,1)} %bitcast.5, bf16[4,256,128]{2,1,0:T(8,128)(2,1)} %bitcast.6, bf16[27,128,128]{2,1,0:T(8,128)(2,1)} %kw_hbm.1, ...), custom_call_target="tpu_custom_call" | custom-call | tf_op jit(solution)/shard_map/step_kernel/pallas_call | solution.py:611
  50.2 1.9 %hand_on.1 = (bf16[4,256,128]{2,1,0:T(8,128)(2,1)}, bf16[4,256,128]{2,1,0:T(8,128)(2,1)}, f32[2,32,63]{2,1,0:T(8,128)}, f32[128,128]{1,0:T(8,128)}, f32[27,2,128]{2,1,0:T(2,128)}) custom-call(bf16[4,256,128]{2,1,0:T(8,128)(2,1)} %get-tuple-element.15.refs_0_, bf16[4,256,128]{2,1,0:T(8,128)(2,1)} %get-tuple-element.16.refs_1_, ...), custom_call_target="tpu_custom_call" | custom-call | tf_op jit(solution)/shard_map/hand_on/pallas_call | solution.py:633
